TPU v7x, 32 devices: a whole 2x2x4 slice. The times are simulated.
32 devices in a mesh: layer: 2 (over core), latent: 16 (over z, y, x).
Axes of the slice: x: 2, y: 2, z: 4, core: 2. Of those that a mesh axis runs over, the one named last changes fastest.
Arguments:
- activations: bfloat16 [2, 512, 2048], P('layer', 'latent'), may hold values from -15 to 15
- enc_weight: bfloat16 [2, 2048, 16384], P('layer', None, 'latent'), may hold values from -0.09375 to 0.09375
- enc_bias: float32 [16384], P('latent'), may hold values from -3 to 3
- dec_weight: bfloat16 [2, 16384, 2048], P('layer', 'latent'), may hold values from -0.1796875 to 0.1796875
- dec_bias: float32 [2, 2048], P('layer'), may hold values from -3 to 3
- active_mask: int32 [512, 16384], P(None, 'latent'), may hold values 0 or 1
Outputs:
- grad_enc: bfloat16 [2, 2048, 16384], P('layer', None, 'latent')
- grad_dec: bfloat16 [2, 16384, 2048], P('layer', 'latent')
- loss_value: float32 [], replicated
All inputs are finite; a program needn't handle non-finite values. No bound on the sum of `active_mask` on one device may be relied on, other than what follows from the above.
Results may differ from a plain program's by a relative error of at most 0.0065.
Values may be sent and summed in bfloat16 or wider, within the bound.
A program may use at most 128 MiB of HBM per device.

v0:
```python
import jax
import jax.numpy as jnp
from jax import lax
from jax.sharding import PartitionSpec as P

sparsity_weight = 0.4


def per_device(activations, enc_weight, enc_bias, dec_weight, dec_bias, active_mask):
    local_rows = activations[0]
    encoder = enc_weight[0]
    decoder = dec_weight[0]
    token_all = lax.all_gather(local_rows, "latent", axis=0, tiled=True)
    layer_pre = jnp.dot(token_all, encoder, preferred_element_type=jnp.float32)
    dec_float = decoder.astype(jnp.float32)
    row_norm = jnp.sqrt(jnp.sum(dec_float * dec_float, axis=1) + 1e-06)
    preact, norm_sum = lax.psum((layer_pre, row_norm), "layer")
    preact = preact + enc_bias
    gating = active_mask.astype(jnp.float32)
    latent_code = preact * gating
    code_b = latent_code.astype(jnp.bfloat16)
    layer_index = lax.axis_index("layer")
    recon_share = (
        lax.psum_scatter(
            jnp.dot(code_b, decoder, preferred_element_type=jnp.float32),
            "latent",
            scatter_dimension=0,
            tiled=True,
        )
        + dec_bias[0]
    )
    error_share = recon_share - local_rows.astype(jnp.float32)
    square_part = 0.5 * jnp.sum(error_share * error_share)
    error_b = lax.all_gather(error_share.astype(jnp.bfloat16), "latent", axis=0, tiled=True)
    layer_grad = jnp.einsum("td,fd->tf", error_b, decoder, preferred_element_type=jnp.float32)
    code_grad = lax.psum(layer_grad, "layer") + sparsity_weight * norm_sum
    preact_grad = (code_grad * gating).astype(jnp.bfloat16)
    grad_enc = jnp.einsum(
        "td,tf->df", token_all, preact_grad, preferred_element_type=jnp.float32
    ).astype(jnp.bfloat16)
    code_total = jnp.sum(latent_code, axis=0)
    shrink = sparsity_weight * code_total[:, None] * dec_float / row_norm[:, None]
    grad_dec = (
        jnp.einsum("tf,td->fd", code_b, error_b, preferred_element_type=jnp.float32) + shrink
    ).astype(jnp.bfloat16)
    sparse_part = jnp.where(
        layer_index == 0, sparsity_weight * jnp.sum(latent_code * norm_sum), 0.0
    )
    loss_total = lax.psum(square_part + sparse_part, ("layer", "latent"))
    loss_value = loss_total / (active_mask.shape[0] * token_all.shape[1])
    return (grad_enc[None], grad_dec[None], loss_value)


def solution(mesh):
    placed = (
        P("layer", "latent", None),
        P("layer", None, "latent"),
        P("latent"),
        P("layer", "latent", None),
        P("layer", None),
        P(None, "latent"),
    )
    return jax.shard_map(
        per_device,
        mesh=mesh,
        in_specs=placed,
        out_specs=(P("layer", None, "latent"), P("layer", "latent", None), P()),
        check_vma=False,
    )
```

profile of v0, /device:TPU:0, one launch (start us, length us, event | category | flops | bytes accessed | tf_op | source)
XLA Modules:
  0.0 342.8 jit_solution(5819471263152638103)
XLA Ops:
  7.2 0.0 all-gather.6.cloned.1.call-start
  7.2 0.7 all-gather.6.cloned.1.call-update
  7.9 0.0 all-reduce.3.cloned.1.call-start
  7.9 65.9 %all-gather.6.cloned.1.call-done = bf16[1,512,2048]{2,1,0:T(8,128)(2,1)} async-done(((bf16[1,32,2048]{2,1,0:T(8,128)(2,1)}), bf16[1,512,2048]{2,1,0:T(8,128)(2,1)}) %all-gather.6.cloned.1.call-update) | async-done | bytes 2097168 | tf_op jit(solution)/shard_map/all_gather | solution.py:13
  73.9 6.5 %fusion.8 = f32[512,1024]{1,0:T(8,128)} fusion(bf16[1,2048,1024]{2,1,0:T(8,128)(2,1)} %param.7, bf16[1,512,2048]{2,1,0:T(8,128)(2,1)} %all-gather.6.cloned.1.call-done), kind=kOutput, calls=%fused_computation.10 | convolution fusion | flops 2147483648 | bytes 8388608 | tf_op jit(solution)/shard_map/dot_general | solution.py:14
  80.4 0.0 all-reduce.3.cloned.1.call-update
  80.4 0.0 copy-start.1
  80.4 0.0 copy-start.4
  80.4 0.0 reduce-scatter.2.cloned.1.call-start
  80.4 3.2 fusion
  83.7 2.5 psum.30
  86.2 14.5 %all-reduce.3.cloned.1.call-done = f32[512,1024]{1,0:T(8,128)} async-done(((f32[512,1024]{1,0:T(8,128)}), f32[512,1024]{1,0:T(8,128)}) %all-reduce.3.cloned.1.call-update) | async-done | bytes 2097168 | tf_op jit(solution)/shard_map/psum | solution.py:17
  100.6 0.0 copy-done.1
  100.6 0.0 copy-done.4
  100.6 0.0 copy-start
  100.6 2.9 multiply_reduce_fusion
  103.6 0.0 copy-done
  103.6 4.4 %fusion.6 = f32[512,2048]{1,0:T(8,128)} fusion(bf16[1,1024,2048]{2,1,0:T(8,128)(2,1)S(1)} %copy-done, bf16[512,1024]{1,0:T(8,128)(2,1)S(1)} %get-tuple-element.8), kind=kOutput, calls=%fused_computation.8 | convolution fusion | flops 2147483648 | bytes 9437184 | tf_op jit(solution)/shard_map/dot_general | solution.py:25
  107.9 0.0 copy-start.2
  107.9 0.0 copy-start.3
  107.9 0.0 reduce-scatter.2.cloned.1.call-update
  108.0 0.0 all-gather.4.cloned.1.call-start
  108.0 96.5 %reduce-scatter.2.cloned.1.call-done = f32[32,2048]{1,0:T(8,128)} async-done(((f32[512,2048]{1,0:T(8,128)}), f32[32,2048]{1,0:T(8,128)}) %reduce-scatter.2.cloned.1.call-update) | async-done | bytes 262160 | tf_op jit(solution)/shard_map/reduce_scatter | solution.py:24
  204.5 0.0 copy-done.2
  204.5 0.0 copy-done.3
  204.5 2.3 multiply_reduce_fusion.1
  206.8 0.0 all-gather.4.cloned.1.call-update
  206.8 0.0 all-reduce.5.cloned.1.call-start
  206.9 60.8 %all-gather.4.cloned.1.call-done = bf16[512,2048]{1,0:T(8,128)(2,1)} async-done(((bf16[32,2048]{1,0:T(8,128)(2,1)}), bf16[512,2048]{1,0:T(8,128)(2,1)}) %all-gather.4.cloned.1.call-update) | async-done | bytes 2097168 | tf_op jit(solution)/shard_map/all_gather | solution.py:34
  267.7 6.5 %fusion.4 = f32[512,1024]{1,0:T(8,128)} fusion(bf16[512,2048]{1,0:T(8,128)(2,1)} %all-gather.4.cloned.1.call-done, bf16[1,1024,2048]{2,1,0:T(8,128)(2,1)} %param.9), kind=kOutput, calls=%fused_computation.6 | convolution fusion | flops 2147483648 | bytes 8388608 | tf_op jit(solution)/shard_map/td,fd->tf/dot_general | solution.py:35
  274.2 0.0 all-reduce.5.cloned.1.call-update
  275.5 39.4 %psum.31 = f32[]{:T(128)} all-reduce(f32[]{:T(128)S(6)} %add.62), channel_id=1, replica_groups=mesh['layer'=2,'latent'=16] {'layer','latent'}, use_global_device_ids=true, to_apply=%region_8.9 | all-reduce | flops 1 | bytes 8 | tf_op jit(solution)/shard_map/psum | solution.py:49
  315.6 6.7 %fusion.10 = bf16[1,1024,2048]{2,1,0:T(8,128)(2,1)} fusion(f32[1024]{0:T(1024)S(1)} %add_sqrt_fusion, bf16[1,1024,2048]{2,1,0:T(8,128)(2,1)} %param.9, f32[1024]{0:T(1024)S(1)} %broadcast_multiply_fusion, bf16[512,2048]{1,0:T(8,128)(2,1)} %all-gather.4.cloned.1.call-done, bf16[512,1024]{1,0:T(8,128)(2,1)S(1)} %get-tuple-element.8), kind=kOutput, calls=%fused_computation.13 | convolution fusion | flops 2157969408 | bytes 11542528 | tf_op jit(solution)/shard_map/tf,td->fd/dot_general | solution.py:44
  322.2 0.0 all-reduce.5.cloned.1.call-done
  322.2 6.5 %convert_bitcast_fusion = bf16[1,2048,1024]{1,2,0:T(8,128)(2,1)} fusion(bf16[1,512,2048]{2,1,0:T(8,128)(2,1)} %all-gather.6.cloned.1.call-done, f32[512,1024]{1,0:T(8,128)} %all-reduce.5.cloned.1.call-done, s32[512,1024]{1,0:T(8,128)S(1)} %copy-done.1, f32[1024]{0:T(1024)S(1)} %broadcast_multiply_fusion.1), kind=kOutput, calls=%fused_computation.12 | convolution fusion | flops 2151677952 | bytes 10489856 | tf_op jit(solution)/shard_map/td,tf->df/dot_general | solution.py:38
  328.8 6.4 %copy.9 = bf16[1,2048,1024]{2,1,0:T(8,128)(2,1)} copy(bf16[1,2048,1024]{1,2,0:T(8,128)(2,1)} %convert_bitcast_fusion) | data formatting | bytes 8388608
  (3 shorter events, 0.0 us)
Async XLA Ops:
  7.2 66.7 %all-gather.6.cloned.1.call-start = ((), (), s32[]{:S(2)}) async-start(), calls=%async_computation.5 | async-start | bytes 2228224 | tf_op jit(solution)/shard_map/all_gather | solution.py:13
  7.9 92.7 %all-reduce.3.cloned.1.call-start = ((), (), s32[]{:S(2)}) async-start(), calls=%async_computation.1 | async-start | bytes 4194304 | tf_op jit(solution)/shard_map/psum | solution.py:17
  80.4 20.3 %copy-start.1 = (s32[512,1024]{1,0:T(8,128)S(1)}, s32[512,1024]{1,0:T(8,128)}, u32[]{:S(2)}) copy-start(s32[512,1024]{1,0:T(8,128)} %param.11) | copy-start | bytes 6291460
  80.4 20.3 %copy-start.4 = (f32[1024]{0:T(1024)S(1)}, f32[1024]{0:T(1024)}, u32[]{:S(2)}) copy-start(f32[1024]{0:T(1024)} %param.8) | copy-start | bytes 12292
  80.4 124.1 %reduce-scatter.2.cloned.1.call-start = ((), (), s32[]{:S(2)}) async-start(), calls=%async_computation.2 | async-start | bytes 4456448 | tf_op jit(solution)/shard_map/reduce_scatter | solution.py:24
  100.6 2.9 copy-start
  107.9 96.6 %copy-start.2 = (bf16[1,32,2048]{2,1,0:T(8,128)(2,1)S(1)}, bf16[1,32,2048]{2,1,0:T(8,128)(2,1)}, u32[]{:S(2)}) copy-start(bf16[1,32,2048]{2,1,0:T(8,128)(2,1)} %param.6) | copy-start | bytes 393220
  107.9 96.6 %copy-start.3 = (f32[1,2048]{1,0:T(1,128)S(1)}, f32[1,2048]{1,0:T(1,128)}, u32[]{:S(2)}) copy-start(f32[1,2048]{1,0:T(1,128)} %param.10) | copy-start | bytes 24580
  108.0 159.7 %all-gather.4.cloned.1.call-start = ((), (), s32[]{:S(2)}) async-start(), calls=%async_computation.3 | async-start | bytes 2228224 | tf_op jit(solution)/shard_map/all_gather | solution.py:34
  206.8 115.4 %all-reduce.5.cloned.1.call-start = ((), (), s32[]{:S(2)}) async-start(), calls=%async_computation.4 | async-start | bytes 4194304 | tf_op jit(solution)/shard_map/psum | solution.py:36
Sparse Core Ops, SparseCore 0:
  10.7 63.0 all-gather.5
  80.5 20.0 all-reduce.2
  108.1 96.3 reduce-scatter.1
  207.7 59.9 all-gather.3
  274.3 20.1 all-reduce.4
where the time goes:
time: 343 us
  waiting for transfers between devices  238 us (69%)
  blocking collectives  41.9 us (12%)
  matrix products  30.6 us (9%)
  between operations  16.9 us (5%)
  other arithmetic  8.39 us (2%)
  local copies, waits for them, and re-layouts  6.41 us (2%)
    reduce_scatter x1, waiting for transfers between devices, per_device(): lax.psum_scatter(jnp.dot(code_b, decoder, preferred_element_type=jnp.floa...  96.5 us
    all_gather x1, waiting for transfers between devices, per_device(): token_all = lax.all_gather(local_rows, 'latent', axis=0, tiled=True)  65.9 us
    all_gather x1, waiting for transfers between devices, per_device(): lax.all_gather(error_share.astype(jnp.bfloat16), 'latent', axis=0, tiled=...  60.8 us
    psum x1, blocking collectives, per_device(): loss_total = lax.psum(square_part + sparse_part, ('layer', 'latent'))  39.4 us
    psum x1, waiting for transfers between devices, per_device(): preact, norm_sum = lax.psum((layer_pre, row_norm), 'layer')  14.5 us
  transfers between devices with their start and end apart: 5, of which 4 were waited for; matrix products, arithmetic and copies ran while one was open for 3% of the time, Pallas kernels for 0%

commit v1 on v0

--- a/solution.py
+++ b/solution.py
@@ -46,7 +46,7 @@
     sparse_part = jnp.where(
         layer_index == 0, sparsity_weight * jnp.sum(latent_code * norm_sum), 0.0
     )
-    loss_total = lax.psum(square_part + sparse_part, ("layer", "latent"))
+    loss_total = jnp.sum(lax.all_gather(square_part + sparse_part, ("layer", "latent")), axis=0)
     loss_value = loss_total / (active_mask.shape[0] * token_all.shape[1])
     return (grad_enc[None], grad_dec[None], loss_value)
 

time: 343 us -> 344 us (level)
    psum x1 -> x0, blocking collectives: 39.4 us -> none  [per_device(): loss_total = lax.psum(square_part + sparse_part, ('layer', 'latent'))]
    unnamed x0 -> x1, blocking collectives: none -> 39.4 us
where the time goes in v1:
time: 344 us
  waiting for transfers between devices  238 us (69%)
  blocking collectives  41.9 us (12%)
  matrix products  30.6 us (9%)
  between operations  16.9 us (5%)
  other arithmetic  8.99 us (3%)
  local copies, waits for them, and re-layouts  6.53 us (2%)
    reduce_scatter x1, waiting for transfers between devices, per_device(): lax.psum_scatter(jnp.dot(code_b, decoder, preferred_element_type=jnp.floa...  96.5 us
    all_gather x1, waiting for transfers between devices, per_device(): token_all = lax.all_gather(local_rows, 'latent', axis=0, tiled=True)  65.9 us
    all_gather x1, waiting for transfers between devices, per_device(): lax.all_gather(error_share.astype(jnp.bfloat16), 'latent', axis=0, tiled=...  60.8 us
    unnamed x1, blocking collectives  39.4 us
    psum x1, waiting for transfers between devices, per_device(): preact, norm_sum = lax.psum((layer_pre, row_norm), 'layer')  14.5 us
  transfers between devices with their start and end apart: 5, of which 4 were waited for; matrix products, arithmetic and copies ran while one was open for 3% of the time, Pallas kernels for 0%

profile of v1, /device:TPU:0, one launch (start us, length us, event | category | flops | bytes accessed | tf_op | source)
XLA Modules:
  0.0 343.5 jit_solution(1318146168340100900)
XLA Ops:
  7.2 0.0 all-gather.6.cloned.1.call-start
  7.2 0.7 all-gather.6.cloned.1.call-update
  7.9 0.0 all-reduce.4.cloned.1.call-start
  7.9 65.9 %all-gather.6.cloned.1.call-done = bf16[1,512,2048]{2,1,0:T(8,128)(2,1)} async-done(((bf16[1,32,2048]{2,1,0:T(8,128)(2,1)}), bf16[1,512,2048]{2,1,0:T(8,128)(2,1)}) %all-gather.6.cloned.1.call-update) | async-done | bytes 2097168 | tf_op jit(solution)/shard_map/all_gather | solution.py:13
  73.9 6.5 %fusion.8 = f32[512,1024]{1,0:T(8,128)} fusion(bf16[1,2048,1024]{2,1,0:T(8,128)(2,1)} %param.7, bf16[1,512,2048]{2,1,0:T(8,128)(2,1)} %all-gather.6.cloned.1.call-done), kind=kOutput, calls=%fused_computation.10 | convolution fusion | flops 2147483648 | bytes 8388608 | tf_op jit(solution)/shard_map/dot_general | solution.py:14
  80.4 0.0 all-reduce.4.cloned.1.call-update
  80.4 0.0 copy-start.1
  80.4 0.0 copy-start.4
  80.4 0.0 reduce-scatter.2.cloned.1.call-start
  80.4 3.2 fusion
  83.7 2.5 psum.23
  86.2 14.5 %all-reduce.4.cloned.1.call-done = f32[512,1024]{1,0:T(8,128)} async-done(((f32[512,1024]{1,0:T(8,128)}), f32[512,1024]{1,0:T(8,128)}) %all-reduce.4.cloned.1.call-update) | async-done | bytes 2097168 | tf_op jit(solution)/shard_map/psum | solution.py:17
  100.6 0.0 copy-done.1
  100.6 0.0 copy-done.4
  100.6 0.0 copy-start
  100.6 2.9 multiply_reduce_fusion
  103.6 0.0 copy-done
  103.6 4.4 %fusion.6 = f32[512,2048]{1,0:T(8,128)} fusion(bf16[1,1024,2048]{2,1,0:T(8,128)(2,1)S(1)} %copy-done, bf16[512,1024]{1,0:T(8,128)(2,1)S(1)} %get-tuple-element.8), kind=kOutput, calls=%fused_computation.8 | convolution fusion | flops 2147483648 | bytes 9437184 | tf_op jit(solution)/shard_map/dot_general | solution.py:25
  107.9 0.0 copy-start.2
  107.9 0.0 copy-start.3
  107.9 0.0 reduce-scatter.2.cloned.1.call-update
  108.0 0.0 all-gather.4.cloned.1.call-start
  108.0 96.5 %reduce-scatter.2.cloned.1.call-done = f32[32,2048]{1,0:T(8,128)} async-done(((f32[512,2048]{1,0:T(8,128)}), f32[32,2048]{1,0:T(8,128)}) %reduce-scatter.2.cloned.1.call-update) | async-done | bytes 262160 | tf_op jit(solution)/shard_map/reduce_scatter | solution.py:24
  204.5 0.0 copy-done.2
  204.5 0.0 copy-done.3
  204.5 2.3 multiply_reduce_fusion.1
  206.8 0.0 all-gather.4.cloned.1.call-update
  206.8 0.0 all-reduce.6.cloned.1.call-start
  206.9 60.8 %all-gather.4.cloned.1.call-done = bf16[512,2048]{1,0:T(8,128)(2,1)} async-done(((bf16[32,2048]{1,0:T(8,128)(2,1)}), bf16[512,2048]{1,0:T(8,128)(2,1)}) %all-gather.4.cloned.1.call-update) | async-done | bytes 2097168 | tf_op jit(solution)/shard_map/all_gather | solution.py:34
  267.7 6.5 %fusion.4 = f32[512,1024]{1,0:T(8,128)} fusion(bf16[512,2048]{1,0:T(8,128)(2,1)} %all-gather.4.cloned.1.call-done, bf16[1,1024,2048]{2,1,0:T(8,128)(2,1)} %param.9), kind=kOutput, calls=%fused_computation.6 | convolution fusion | flops 2147483648 | bytes 8388608 | tf_op jit(solution)/shard_map/td,fd->tf/dot_general | solution.py:35
  274.2 0.0 all-reduce.6.cloned.1.call-update
  275.5 0.1 dynamic-update-slice
  275.6 39.4 %all-reduce = f32[32]{0:T(128)S(1)} all-reduce(f32[32]{0:T(128)S(1)} %dynamic-update-slice), channel_id=1, replica_groups=mesh['layer'=2,'latent'=16] {'layer','latent'}, use_global_device_ids=true, to_apply=%add | all-reduce | flops 32 | bytes 256
  315.0 0.6 reduce_sum.49
  316.3 6.7 %fusion.10 = bf16[1,1024,2048]{2,1,0:T(8,128)(2,1)} fusion(f32[1024]{0:T(1024)S(1)} %add_sqrt_fusion, bf16[1,1024,2048]{2,1,0:T(8,128)(2,1)} %param.9, f32[1024]{0:T(1024)S(1)} %broadcast_multiply_fusion, bf16[512,2048]{1,0:T(8,128)(2,1)} %all-gather.4.cloned.1.call-done, bf16[512,1024]{1,0:T(8,128)(2,1)S(1)} %get-tuple-element.8), kind=kOutput, calls=%fused_computation.13 | convolution fusion | flops 2157969408 | bytes 11542528 | tf_op jit(solution)/shard_map/tf,td->fd/dot_general | solution.py:44
  322.9 0.0 all-reduce.6.cloned.1.call-done
  322.9 6.5 %convert_bitcast_fusion = bf16[1,2048,1024]{1,2,0:T(8,128)(2,1)} fusion(bf16[1,512,2048]{2,1,0:T(8,128)(2,1)} %all-gather.6.cloned.1.call-done, f32[512,1024]{1,0:T(8,128)} %all-reduce.6.cloned.1.call-done, s32[512,1024]{1,0:T(8,128)S(1)} %copy-done.1, f32[1024]{0:T(1024)S(1)} %broadcast_multiply_fusion.1), kind=kOutput, calls=%fused_computation.12 | convolution fusion | flops 2151677952 | bytes 10489856 | tf_op jit(solution)/shard_map/td,tf->df/dot_general | solution.py:38
  329.5 6.4 %copy.9 = bf16[1,2048,1024]{2,1,0:T(8,128)(2,1)} copy(bf16[1,2048,1024]{1,2,0:T(8,128)(2,1)} %convert_bitcast_fusion) | data formatting | bytes 8388608
  (4 shorter events, 0.0 us)
Async XLA Ops:
  7.2 66.7 %all-gather.6.cloned.1.call-start = ((), (), s32[]{:S(2)}) async-start(), calls=%async_computation.5 | async-start | bytes 2228224 | tf_op jit(solution)/shard_map/all_gather | solution.py:13
  7.9 92.7 %all-reduce.4.cloned.1.call-start = ((), (), s32[]{:S(2)}) async-start(), calls=%async_computation.1 | async-start | bytes 4194304 | tf_op jit(solution)/shard_map/psum | solution.py:17
  80.4 20.3 %copy-start.1 = (s32[512,1024]{1,0:T(8,128)S(1)}, s32[512,1024]{1,0:T(8,128)}, u32[]{:S(2)}) copy-start(s32[512,1024]{1,0:T(8,128)} %param.11) | copy-start | bytes 6291460
  80.4 20.3 %copy-start.4 = (f32[1024]{0:T(1024)S(1)}, f32[1024]{0:T(1024)}, u32[]{:S(2)}) copy-start(f32[1024]{0:T(1024)} %param.8) | copy-start | bytes 12292
  80.4 124.1 %reduce-scatter.2.cloned.1.call-start = ((), (), s32[]{:S(2)}) async-start(), calls=%async_computation.2 | async-start | bytes 4456448 | tf_op jit(solution)/shard_map/reduce_scatter | solution.py:24
  100.6 2.9 copy-start
  107.9 96.6 %copy-start.2 = (bf16[1,32,2048]{2,1,0:T(8,128)(2,1)S(1)}, bf16[1,32,2048]{2,1,0:T(8,128)(2,1)}, u32[]{:S(2)}) copy-start(bf16[1,32,2048]{2,1,0:T(8,128)(2,1)} %param.6) | copy-start | bytes 393220
  107.9 96.6 %copy-start.3 = (f32[1,2048]{1,0:T(1,128)S(1)}, f32[1,2048]{1,0:T(1,128)}, u32[]{:S(2)}) copy-start(f32[1,2048]{1,0:T(1,128)} %param.10) | copy-start | bytes 24580
  108.0 159.7 %all-gather.4.cloned.1.call-start = ((), (), s32[]{:S(2)}) async-start(), calls=%async_computation.3 | async-start | bytes 2228224 | tf_op jit(solution)/shard_map/all_gather | solution.py:34
  206.8 116.1 %all-reduce.6.cloned.1.call-start = ((), (), s32[]{:S(2)}) async-start(), calls=%async_computation.4 | async-start | bytes 4194304 | tf_op jit(solution)/shard_map/psum | solution.py:36
Sparse Core Ops, SparseCore 0:
  10.7 63.0 all-gather.5
  80.5 20.0 all-reduce.3
  108.1 96.3 reduce-scatter.1
  207.7 59.9 all-gather.3
  274.3 20.0 all-reduce.5
